TPU v7x, 32 devices: a whole 2x2x4 slice. The times are simulated.
32 devices in a mesh: dp: 4 (over y, core), mp: 8 (over z, x).
Axes of the slice: x: 2, y: 2, z: 4, core: 2. Of those that a mesh axis runs over, the one named last changes fastest.
Arguments:
- pair_tokens: bfloat16 [64, 48, 8192], P('dp', None, 'mp'), may hold values from -6 to 6
- norm_gain: float32 [8192], replicated, may hold values from 0.1 to 1.9
- q_weight: bfloat16 [8192, 4096], P('dp', 'mp'), may hold values from -1.5 to 1.5
- k_weight: bfloat16 [8192, 1024], P('dp', 'mp'), may hold values from -1.5 to 1.5
- value_weight: bfloat16 [8192, 1024], P('dp', 'mp'), may hold values from -0.0625 to 0.0625
- o_weight: bfloat16 [4096, 8192], P('mp', 'dp'), may hold values from -0.375 to 0.375
- pair_row: int32 [64], replicated, may hold values from 0 to 15, as said below
- pair_span: int32 [64, 2], replicated, may hold values from 0 to 128, as said below
- block_ids: int32 [2048], P('dp'), may hold values from 0 to 11, as said below
Outputs:
- attn_out: bfloat16 [2048, 8192], P('dp', 'mp')
Inputs may be any that keep to these rules, and one draw needn't show every extreme that they name: `pair_row`: every packed row is tiled exactly by the spans of the pairs that name it; the pairs listed on one index of dp that name rows of one index of dp number at most 4, and 4 is reached. `pair_span`: each span holds one pair, start before end; end - start is at least 3 and at most 48; 48 is reached in every row, and the last pair of every row ends at 128. `block_ids`: the pair's place counts the pairs of its row in order of position; roles are 0 prompt, 1 chosen, 2 rejected, in that order within each pair, each present; consistent with pair_row and pair_span.
All inputs are finite; a program needn't handle non-finite values.
Results may differ from a plain program's by a relative error of at most 0.013.
Values may be sent and summed in bfloat16 or wider, within the bound.
A program may use at most 128 MiB of HBM per device.

v0:
```python
import jax
import jax.numpy as jnp
from jax import lax
from jax.sharding import PartitionSpec as P

HEAD_SIZE = 128
ROW_TOKENS = 128
QUERY_PER_KV = 4


def apply_rotary(values, token_position, heads):
    half = HEAD_SIZE // 2
    freq = 500000.0 ** (-(jnp.arange(half, dtype=jnp.float32) * 2.0 / HEAD_SIZE))
    angle = token_position.astype(jnp.float32)[:, None] * freq[None, :]
    cosine = jnp.cos(angle)[:, None, :]
    sine = jnp.sin(angle)[:, None, :]
    shaped = values.reshape(values.shape[0], heads, HEAD_SIZE)
    first = shaped[..., :half]
    second = shaped[..., half:]
    turned = jnp.concatenate(
        [first * cosine - second * sine, second * cosine + first * sine], axis=-1
    )
    return turned.reshape(values.shape[0], heads * HEAD_SIZE).astype(jnp.bfloat16)


def row_mask(ids):
    pair_of = ids // 3
    role_of = ids % 3
    steps_a = jnp.arange(ids.shape[0])
    causal = steps_a[None, :] <= steps_a[:, None]
    same = pair_of[:, None] == pair_of[None, :]
    hidden_pair = (role_of[:, None] == 2) & (role_of[None, :] == 1)
    return causal & same & jnp.logical_not(hidden_pair)


def local(
    pair_tokens,
    norm_gain,
    q_weight,
    k_weight,
    value_weight,
    o_weight,
    pair_row,
    pair_span,
    block_ids,
):
    dp_count = lax.axis_size("dp")
    own_index = lax.axis_index("dp")
    pairs_dev = pair_tokens.shape[0]
    pair_cap = pair_tokens.shape[1]
    width_local = pair_tokens.shape[2]
    all_pairs = pair_row.shape[0]
    most_sent = -(-pairs_dev // dp_count)
    tok_dev = block_ids.shape[0]
    rows_dev = tok_dev // ROW_TOKENS
    owners_all = (pair_row // rows_dev).reshape(dp_count, pairs_dev)
    same_owner = owners_all[:, :, None] == owners_all[:, None, :]
    listed = jnp.arange(pairs_dev)
    before = listed[None, :] < listed[:, None]
    rank_all = jnp.sum((same_owner & before[None]).astype(jnp.int32), axis=2)
    own_owner = lax.dynamic_index_in_dim(owners_all, own_index, 0, keepdims=False)
    own_rank = lax.dynamic_index_in_dim(rank_all, own_index, 0, keepdims=False)
    outgoing = jnp.zeros((dp_count * most_sent, pair_cap, width_local), jnp.bfloat16)
    outgoing = outgoing.at[own_owner * most_sent + own_rank].set(pair_tokens)
    incoming = lax.all_to_all(
        outgoing.reshape(dp_count, most_sent * pair_cap, width_local),
        "dp",
        split_axis=0,
        concat_axis=0,
        tiled=True,
    )
    slots = jnp.arange(pair_cap, dtype=jnp.int32)
    length = pair_span[:, 1] - pair_span[:, 0]
    source = jnp.arange(all_pairs, dtype=jnp.int32) // pairs_dev
    target = (pair_row % rows_dev)[:, None] * ROW_TOKENS + pair_span[:, 0][:, None] + slots[None, :]
    usable = (owners_all.reshape(-1) == own_index)[:, None] & (slots[None, :] < length[:, None])
    slot_index = (source * most_sent + rank_all.reshape(-1))[:, None] * pair_cap + slots[None, :]
    buffer_size = dp_count * most_sent * pair_cap
    slot_index = jnp.where(usable, slot_index, buffer_size)
    placement_map = jnp.full((buffer_size,), tok_dev, jnp.int32)
    placement_map = placement_map.at[slot_index.reshape(-1)].set(target.reshape(-1), mode="drop")
    packed_local = jnp.zeros((tok_dev, width_local), jnp.bfloat16)
    packed_local = packed_local.at[placement_map].set(
        incoming.reshape(buffer_size, width_local), mode="drop"
    )
    packed = lax.all_gather(packed_local, "mp", axis=1, tiled=True)
    wide = packed.astype(jnp.float32)
    scale = lax.rsqrt(jnp.mean(wide * wide, axis=-1, keepdims=True) + 1e-05)
    normed = (wide * scale * norm_gain[None, :]).astype(jnp.bfloat16)

    def add_rows(piece):
        return jnp.dot(normed, piece, preferred_element_type=jnp.float32)

    query_heads = add_rows(lax.all_gather(q_weight, "dp", axis=0, tiled=True))
    key_rows = add_rows(lax.all_gather(k_weight, "dp", axis=0, tiled=True))
    value_sum = add_rows(lax.all_gather(value_weight, "dp", axis=0, tiled=True))
    value_heads = value_sum.astype(jnp.bfloat16)
    ids_rows = block_ids.reshape(rows_dev, ROW_TOKENS)
    visible = jax.vmap(row_mask)(ids_rows)
    token_position = (jnp.sum(visible.astype(jnp.int32), axis=2) - 1).reshape(tok_dev)
    kv_local = k_weight.shape[1] // HEAD_SIZE
    q_local = q_weight.shape[1] // HEAD_SIZE
    rotated_query = apply_rotary(query_heads, token_position, q_local).reshape(
        rows_dev, ROW_TOKENS, kv_local, QUERY_PER_KV, HEAD_SIZE
    )
    rotated_key = apply_rotary(key_rows, token_position, kv_local).reshape(
        rows_dev, ROW_TOKENS, kv_local, HEAD_SIZE
    )
    v_rows = value_heads.reshape(rows_dev, ROW_TOKENS, kv_local, HEAD_SIZE)
    scores = jnp.einsum(
        "rihgd,rjhd->rhgij", rotated_query, rotated_key, preferred_element_type=jnp.float32
    ) * HEAD_SIZE ** (-0.5)
    scores = jnp.where(visible[:, None, None], scores, -1e30)
    top = jnp.max(scores, axis=-1, keepdims=True)
    expo = jnp.exp(scores - top)
    probs = (expo / jnp.sum(expo, axis=-1, keepdims=True)).astype(jnp.bfloat16)
    attn = jnp.einsum(
        "rhgij,rjhd->rihgd", probs, v_rows, preferred_element_type=jnp.float32
    ).astype(jnp.bfloat16)
    attn = attn.reshape(tok_dev, q_local * HEAD_SIZE)
    terms = jnp.dot(
        attn, lax.all_gather(o_weight, "dp", axis=1, tiled=True), preferred_element_type=jnp.float32
    )
    return lax.psum_scatter(terms.astype(jnp.bfloat16), "mp", scatter_dimension=1, tiled=True)


def solution(mesh):
    placed = (
        P("dp", None, "mp"),
        P(),
        P("dp", "mp"),
        P("dp", "mp"),
        P("dp", "mp"),
        P("mp", "dp"),
        P(),
        P(),
        P("dp"),
    )
    return jax.shard_map(
        local, mesh=mesh, in_specs=placed, out_specs=P("dp", "mp"), check_vma=False
    )
```

profile of v0, /device:TPU:0, one launch (start us, length us, event | category | flops | bytes accessed | tf_op | source)
XLA Modules:
  0.0 501.9 jit_solution(16550077983021786801)
XLA Ops:
  6.6 0.7 broadcast_compare_fusion.2
  7.6 1.3 broadcast_in_dim.24
  8.9 5.4 %scatter_fusion = bf16[16,48,1024]{2,1,0:T(8,128)(2,1)} fusion(bf16[16,48,1024]{2,1,0:T(8,128)(2,1)} %broadcast_in_dim.24, s32[16]{0:T(128)S(1)} %fusion.33, bf16[16,48,1024]{2,1,0:T(8,128)(2,1)} %param.9), kind=kCustom, calls=%fused_computation.1 | custom fusion | bytes 4718656 | tf_op jit(solution)/shard_map/scatter | solution.py:64
  14.4 4.3 all-to-all-start
  19.1 11.8 %scatter_custom_fusion = s32[768]{0:T(1024)S(1)} fusion(s32[3072]{0:T(1024)S(1)} %bitcast.87, s32[3072]{0:T(1024)S(1)} %reshape.406, s32[]{:T(128)} %constant.90.clone.1), kind=kCustom, calls=%fused_computation.60 | custom fusion | bytes 3076 | tf_op jit(solution)/shard_map/scatter | solution.py:81
  30.9 7.8 %all-to-all-done = bf16[4,192,1024]{2,1,0:T(8,128)(2,1)S(1)} async-done(((bf16[4,192,1024]{2,1,0:T(8,128)(2,1)}), bf16[4,192,1024]{2,1,0:T(8,128)(2,1)S(1)}, u32[]{:S(2)}, u32[]{:S(2)}) %all-to-all-start) | async-done | bytes 1572896 | tf_op jit(solution)/shard_map/all_to_all | solution.py:65
  38.7 6.7 %scatter_custom_fusion.2 = bf16[512,1024]{1,0:T(8,128)(2,1)} fusion(s32[768]{0:T(1024)S(1)} %compare_select_fusion.1, bf16[768,1024]{1,0:T(8,128)(2,1)S(1)} %bitcast.83, bf16[]{:T(256)} %constant.89.clone.1), kind=kCustom, calls=%fused_computation.26 | custom fusion | bytes 1048578 | tf_op jit(solution)/shard_map/scatter | solution.py:83
  45.4 0.7 all-gather.12.cloned.1.call-update
  46.1 0.7 all-gather.10.cloned.1.call-update
  46.9 0.5 all-gather.8.cloned.1.call-update
  47.5 0.5 all-gather.14.cloned.1.call-update
  48.4 1.0 multiply_cosine_fusion
  49.4 121.7 %all-gather.6.cloned.1.call-done = bf16[512,8192]{1,0:T(8,128)(2,1)} async-done(((bf16[512,1024]{1,0:T(8,128)(2,1)}), bf16[512,8192]{1,0:T(8,128)(2,1)}) %all-gather.6.cloned.1.call-update) | async-done | bytes 8388624 | tf_op jit(solution)/shard_map/all_gather | solution.py:86
  171.0 5.1 %fusion = f32[512]{0:T(512)S(1)} fusion(bf16[512,8192]{1,0:T(8,128)(2,1)} %all-gather.6.cloned.1.call-done), kind=kLoop, calls=%fused_computation.5 | loop fusion | flops 12582400 | bytes 8390656 | tf_op jit(solution)/shard_map/reduce_sum | solution.py:88
  176.1 52.9 %all-gather.12.cloned.1.call-done = bf16[8192,512]{1,0:T(8,128)(2,1)} async-done(((bf16[2048,512]{1,0:T(8,128)(2,1)}), bf16[8192,512]{1,0:T(8,128)(2,1)}) %all-gather.12.cloned.1.call-update) | async-done | bytes 8388624 | tf_op jit(solution)/shard_map/all_gather | solution.py:94
  229.0 11.4 %fusion.35 = f32[512,512]{0,1:T(8,128)S(1)} fusion(bf16[8192,512]{1,0:T(8,128)(2,1)} %all-gather.12.cloned.1.call-done, bf16[512,8192]{1,0:T(8,128)(2,1)} %all-gather.6.cloned.1.call-done, f32[8192]{0:T(1024)S(1)} %copy-done.3, f32[512]{0:T(512)S(1)} %add_rsqrt_fusion), kind=kOutput, calls=%fused_computation.87 | convolution fusion | flops 4311744512 | bytes 17860608 | tf_op jit(solution)/shard_map/dot_general | solution.py:92
  241.2 12.1 %all-gather.10.cloned.1.call-done = bf16[8192,128]{1,0:T(8,128)(2,1)} async-done(((bf16[2048,128]{1,0:T(8,128)(2,1)}), bf16[8192,128]{1,0:T(8,128)(2,1)}) %all-gather.10.cloned.1.call-update) | async-done | bytes 2097168 | tf_op jit(solution)/shard_map/all_gather | solution.py:95
  253.2 6.5 %convolution_bitcast_fusion = f32[512,1,128]{0,2,1:T(8,128)S(1)} fusion(bf16[8192,128]{1,0:T(8,128)(2,1)} %all-gather.10.cloned.1.call-done, bf16[512,8192]{1,0:T(8,128)(2,1)} %all-gather.6.cloned.1.call-done, f32[8192]{0:T(1024)S(1)} %copy-done.3, f32[512]{0:T(512)S(1)} %add_rsqrt_fusion), kind=kOutput, calls=%fused_computation.14 | convolution fusion | flops 1090519040 | bytes 10782720 | tf_op jit(solution)/shard_map/dot_general | solution.py:92
  259.7 0.6 fusion.18
  261.5 15.7 %all-gather.8.cloned.1.call-done = bf16[8192,128]{1,0:T(8,128)(2,1)} async-done(((bf16[2048,128]{1,0:T(8,128)(2,1)}), bf16[8192,128]{1,0:T(8,128)(2,1)}) %all-gather.8.cloned.1.call-update) | async-done | bytes 2097168 | tf_op jit(solution)/shard_map/all_gather | solution.py:96
  277.2 6.4 %convolution_convert_fusion.2 = bf16[512,128]{1,0:T(8,128)(2,1)S(1)} fusion(bf16[8192,128]{1,0:T(8,128)(2,1)} %all-gather.8.cloned.1.call-done, bf16[512,8192]{1,0:T(8,128)(2,1)} %all-gather.6.cloned.1.call-done, f32[8192]{0:T(1024)S(1)} %copy-done.3, f32[512]{0:T(512)S(1)} %add_rsqrt_fusion), kind=kOutput, calls=%fused_computation.15 | convolution fusion | flops 1090584576 | bytes 10651648 | tf_op jit(solution)/shard_map/dot_general | solution.py:92
  284.3 52.7 %all-gather.14.cloned.1.call-done = bf16[512,8192]{1,0:T(8,128)(2,1)} async-done(((bf16[512,2048]{1,0:T(8,128)(2,1)}), bf16[512,8192]{1,0:T(8,128)(2,1)}) %all-gather.14.cloned.1.call-update) | async-done | bytes 8388624 | tf_op jit(solution)/shard_map/all_gather | solution.py:122
  336.9 10.1 %convolution_convert_fusion = bf16[512,8192]{1,0:T(8,128)(2,1)} fusion(bf16[512,8192]{1,0:T(8,128)(2,1)} %all-gather.14.cloned.1.call-done, bf16[64,8,4,128]{3,2,1,0:T(4,128)(2,1)S(1)} %bitcast.86), kind=kOutput, calls=%fused_computation.8 | convolution fusion | flops 4299161600 | bytes 17301504 | tf_op jit(solution)/shard_map/dot_general | solution.py:121
  347.0 148.0 %reduce-scatter.2.cloned.1.call-done = bf16[512,1024]{1,0:T(8,128)(2,1)} async-done(((bf16[512,8192]{1,0:T(8,128)(2,1)}), bf16[512,1024]{1,0:T(8,128)(2,1)}) %reduce-scatter.2.cloned.1.call-update) | async-done | bytes 1048592 | tf_op jit(solution)/shard_map/reduce_scatter | solution.py:124
  (47 shorter events, 3.9 us)
Async XLA Ops:
  6.5 12.2 %copy-start.1 = (s32[64]{0:T(128)S(1)}, s32[64]{0:T(128)}, u32[]{:S(2)}) copy-start(s32[64]{0:T(128)} %param.15) | copy-start | bytes 772
  6.5 12.2 %copy-start.2 = (s32[64,2]{0,1:T(2,128)S(1)}, s32[64,2]{0,1:T(2,128)}, u32[]{:S(2)}) copy-start(s32[64,2]{0,1:T(2,128)} %param.16) | copy-start | bytes 1540
  7.6 40.5 %copy-start = (s32[512]{0:T(512)S(1)}, s32[512]{0:T(512)}, u32[]{:S(2)}) copy-start(s32[512]{0:T(512)} %param.17) | copy-start | bytes 6148
  14.4 24.3 %all-to-all-start = ((bf16[4,192,1024]{2,1,0:T(8,128)(2,1)}), bf16[4,192,1024]{2,1,0:T(8,128)(2,1)S(1)}, u32[]{:S(2)}, u32[]{:S(2)}) async-start(bf16[4,192,1024]{2,1,0:T(8,128)(2,1)} %bitcast.6), calls=%async_computation | async-start | bytes 3145728 | tf_op jit(solution)/shard_map/all_to_all | solution.py:65
  18.6 210.4 %copy-start.3 = (f32[8192]{0:T(1024)S(1)}, f32[8192]{0:T(1024)}, u32[]{:S(2)}) copy-start(f32[8192]{0:T(1024)} %param.10) | copy-start | bytes 98308
  18.6 152.4 %all-gather.6.cloned.1.call-start = ((), (), s32[]{:S(2)}) async-start(), calls=%async_computation.2 | async-start | bytes 9437184 | tf_op jit(solution)/shard_map/all_gather | solution.py:86
  45.3 183.7 %all-gather.12.cloned.1.call-start = ((), (), s32[]{:S(2)}) async-start(), calls=%async_computation.5 | async-start | bytes 10485760 | tf_op jit(solution)/shard_map/all_gather | solution.py:94
  46.1 207.1 %all-gather.10.cloned.1.call-start = ((), (), s32[]{:S(2)}) async-start(), calls=%async_computation.4 | async-start | bytes 2621440 | tf_op jit(solution)/shard_map/all_gather | solution.py:95
  46.8 230.4 %all-gather.8.cloned.1.call-start = ((), (), s32[]{:S(2)}) async-start(), calls=%async_computation.3 | async-start | bytes 2621440 | tf_op jit(solution)/shard_map/all_gather | solution.py:96
  47.4 289.5 %all-gather.14.cloned.1.call-start = ((), (), s32[]{:S(2)}) async-start(), calls=%async_computation.6 | async-start | bytes 10485760 | tf_op jit(solution)/shard_map/all_gather | solution.py:122
  48.0 447.0 %reduce-scatter.2.cloned.1.call-start = ((), (), s32[]{:S(2)}) async-start(), calls=%async_computation.7 | async-start | bytes 9437184 | tf_op jit(solution)/shard_map/reduce_scatter | solution.py:124
Sparse Core Ops, SparseCore 0:
  45.5 125.4 all-gather.5
  172.6 56.4 all-gather.11
  230.6 22.5 all-gather.9
  254.7 22.5 all-gather.7
  278.6 58.2 all-gather.13
  347.2 147.8 reduce-scatter.1
where the time goes:
time: 502 us
  waiting for transfers between devices  413 us (82%)
  matrix products  35 us (7%)
  local copies, waits for them, and re-layouts  26.7 us (5%)
  between operations  13.7 us (3%)
  other arithmetic  8.88 us (2%)
    reduce_scatter x1, waiting for transfers between devices, local(): lax.psum_scatter(terms.astype(jnp.bfloat16), 'mp', scatter_dimension=1, t...  148 us
    all_gather x1, waiting for transfers between devices, local(): packed = lax.all_gather(packed_local, 'mp', axis=1, tiled=True)  122 us
    all_gather x1, waiting for transfers between devices, local(): query_heads = add_rows(lax.all_gather(q_weight, 'dp', axis=0, tiled=True))  52.9 us
    all_gather x1, waiting for transfers between devices, local(): lax.all_gather(o_weight, 'dp', axis=1, tiled=True)  52.7 us
    dot_general x3, matrix products, add_rows(): return jnp.dot(normed, piece, preferred_element_type=jnp.float32)  24.2 us
    all_gather x1, waiting for transfers between devices, local(): value_sum = add_rows(lax.all_gather(value_weight, 'dp', axis=0, tiled=True))  15.7 us
    all_gather x1, waiting for transfers between devices, local(): key_rows = add_rows(lax.all_gather(k_weight, 'dp', axis=0, tiled=True))  12.1 us
    scatter x1, local copies, waits for them, and re-layouts, local(): placement_map.at[slot_index.reshape(-1)]  11.8 us
  transfers between devices with their start and end apart: 7, of which 7 were waited for; matrix products, arithmetic and copies ran while one was open for 9% of the time, Pallas kernels for 0%

commit v1 on v0

--- a/solution.py
+++ b/solution.py
@@ -83,7 +83,14 @@
     packed_local = packed_local.at[placement_map].set(
         incoming.reshape(buffer_size, width_local), mode="drop"
     )
-    packed = lax.all_gather(packed_local, "mp", axis=1, tiled=True)
+    size = lax.axis_size("mp")
+    right = [(i, (i + 1) % size) for i in range(size)]
+    parts = [packed_local]
+    for far in range(1, size):
+        parts = [lax.ppermute(parts[0], "mp", right), *parts]
+    out = jnp.concatenate(parts, axis=1)
+    shift = (lax.axis_index("mp") + 1) * parts[-1].shape[1]
+    packed = jnp.roll(out, shift, axis=1)
     wide = packed.astype(jnp.float32)
     scale = lax.rsqrt(jnp.mean(wide * wide, axis=-1, keepdims=True) + 1e-05)
     normed = (wide * scale * norm_gain[None, :]).astype(jnp.bfloat16)

time: 502 us -> 444 us (0.88)
  waiting for transfers between devices: 413 us -> 334 us
  local copies, waits for them, and re-layouts: 26.7 us -> 44.8 us
    ppermute x0 -> x7, waiting for transfers between devices: none -> 171 us  [local(): parts = [lax.ppermute(parts[0], 'mp', right), *parts]]
    all_gather x1 -> x0, waiting for transfers between devices: 122 us -> none  [local(): packed = lax.all_gather(packed_local, 'mp', axis=1, tiled=True)]
    all_gather x1, waiting for transfers between devices: 52.9 us -> 0.01 us  [local(): query_heads = add_rows(lax.all_gather(q_weight, 'dp', axis=0, tiled=True))]
    all_gather x1, waiting for transfers between devices: 52.7 us -> 0.02 us  [local(): lax.all_gather(o_weight, 'dp', axis=1, tiled=True)]
    unnamed x10 -> x35, local copies, waits for them, and re-layouts: 0.68 us -> 19.3 us
    all_gather x1, waiting for transfers between devices: 15.7 us -> 0.02 us  [local(): value_sum = add_rows(lax.all_gather(value_weight, 'dp', axis=0, tiled=True))]
    all_gather x1, waiting for transfers between devices: 12.1 us -> 0.02 us  [local(): key_rows = add_rows(lax.all_gather(k_weight, 'dp', axis=0, tiled=True))]
    all_to_all x1, waiting for transfers between devices: 7.76 us -> 15.6 us  [local(): lax.all_to_all(outgoing.reshape(dp_count, most_sent * pair_cap, width_loc...]
  transfers between devices with their start and end apart: 7 -> 13, of which waited for: 7 -> 9; matrix products, arithmetic and copies ran while one was open for 9% -> 16% of each run, Pallas kernels for 0% -> 0%
where the time goes in v1:
time: 444 us
  waiting for transfers between devices  334 us (75%)
  local copies, waits for them, and re-layouts  44.8 us (10%)
  matrix products  36.8 us (8%)
  between operations  13.6 us (3%)
  other arithmetic  8.45 us (2%)
  starting transfers between devices  5.9 us (1%)
    ppermute x7, waiting for transfers between devices, local(): parts = [lax.ppermute(parts[0], 'mp', right), *parts]  171 us
    reduce_scatter x1, waiting for transfers between devices, local(): lax.psum_scatter(terms.astype(jnp.bfloat16), 'mp', scatter_dimension=1, t...  145 us
    dot_general x3, matrix products, add_rows(): return jnp.dot(normed, piece, preferred_element_type=jnp.float32)  25.1 us
    unnamed x35, local copies, waits for them, and re-layouts  19.3 us
    all_to_all x1, waiting for transfers between devices, local(): lax.all_to_all(outgoing.reshape(dp_count, most_sent * pair_cap, width_loc...  15.6 us
    scatter x1, local copies, waits for them, and re-layouts, local(): placement_map.at[slot_index.reshape(-1)]  11.8 us
    dot_general x1, matrix products, local(): jnp.dot(attn, lax.all_gather(o_weight, 'dp', axis=1, tiled=True), preferr...  10.1 us
  transfers between devices with their start and end apart: 13, of which 9 were waited for; matrix products, arithmetic and copies ran while one was open for 16% of the time, Pallas kernels for 0%

profile of v1, /device:TPU:0, one launch (start us, length us, event | category | flops | bytes accessed | tf_op | source)
XLA Modules:
  0.0 443.7 jit_solution(17201823302153776601)
XLA Ops:
  9.7 1.4 broadcast_in_dim.24
  11.2 5.5 %scatter_fusion = bf16[16,48,1024]{2,1,0:T(8,128)(2,1)} fusion(bf16[16,48,1024]{2,1,0:T(8,128)(2,1)} %broadcast_in_dim.24, s32[16]{0:T(128)S(1)} %fusion.35, bf16[16,48,1024]{2,1,0:T(8,128)(2,1)} %param.9), kind=kCustom, calls=%fused_computation.1 | custom fusion | bytes 4718656 | tf_op jit(solution)/shard_map/scatter | solution.py:64
  16.6 4.2 all-to-all-start
  22.1 11.8 %scatter_custom_fusion = s32[768]{0:T(1024)S(1)} fusion(s32[3072]{0:T(1024)S(1)} %bitcast.87, s32[3072]{0:T(1024)S(1)} %reshape.406, s32[]{:T(128)} %constant.112.clone.1), kind=kCustom, calls=%fused_computation.76 | custom fusion | bytes 3076 | tf_op jit(solution)/shard_map/scatter | solution.py:81
  33.9 15.6 %all-to-all-done = bf16[4,192,1024]{2,1,0:T(8,128)(2,1)S(1)} async-done(((bf16[4,192,1024]{2,1,0:T(8,128)(2,1)}), bf16[4,192,1024]{2,1,0:T(8,128)(2,1)S(1)}, u32[]{:S(2)}, u32[]{:S(2)}) %all-to-all-start) | async-done | bytes 1572896 | tf_op jit(solution)/shard_map/all_to_all | solution.py:65
  49.5 5.9 %scatter_custom_fusion.2 = bf16[512,1024]{1,0:T(8,128)(2,1)S(1)} fusion(s32[768]{0:T(1024)S(1)} %compare_select_fusion.1, bf16[768,1024]{1,0:T(8,128)(2,1)S(1)} %bitcast.83, bf16[]{:T(256)} %constant.111.clone.1), kind=kCustom, calls=%fused_computation.26 | custom fusion | bytes 1048578 | tf_op jit(solution)/shard_map/scatter | solution.py:83
  55.5 1.5 collective-permute-start
  57.0 26.2 %collective-permute-done = bf16[512,1024]{1,0:T(8,128)(2,1)S(1)} collective-permute-done((bf16[512,1024]{1,0:T(8,128)(2,1)S(1)}, bf16[512,1024]{1,0:T(8,128)(2,1)S(1)}, u32[]{:S(2)}, u32[]{:S(2)}) %collective-permute-start) | collective-permute-done | bytes 1048608 | tf_op jit(solution)/shard_map/ppermute | solution.py:90
  83.3 26.7 %collective-permute-done.1 = bf16[512,1024]{1,0:T(8,128)(2,1)S(1)} collective-permute-done((bf16[512,1024]{1,0:T(8,128)(2,1)S(1)}, bf16[512,1024]{1,0:T(8,128)(2,1)S(1)}, u32[]{:S(2)}, u32[]{:S(2)}) %collective-permute-start.1) | collective-permute-done | bytes 1048608 | tf_op jit(solution)/shard_map/ppermute | solution.py:90
  110.0 25.9 %collective-permute-done.2 = bf16[512,1024]{1,0:T(8,128)(2,1)S(1)} collective-permute-done((bf16[512,1024]{1,0:T(8,128)(2,1)S(1)}, bf16[512,1024]{1,0:T(8,128)(2,1)S(1)}, u32[]{:S(2)}, u32[]{:S(2)}) %collective-permute-start.2) | collective-permute-done | bytes 1048608 | tf_op jit(solution)/shard_map/ppermute | solution.py:90
  136.9 25.1 %collective-permute-done.3 = bf16[512,1024]{1,0:T(8,128)(2,1)S(1)} collective-permute-done((bf16[512,1024]{1,0:T(8,128)(2,1)S(1)}, bf16[512,1024]{1,0:T(8,128)(2,1)S(1)}, u32[]{:S(2)}, u32[]{:S(2)}) %collective-permute-start.3) | collective-permute-done | bytes 1048608 | tf_op jit(solution)/shard_map/ppermute | solution.py:90
  163.0 24.2 %collective-permute-done.4 = bf16[512,1024]{1,0:T(8,128)(2,1)S(1)} collective-permute-done((bf16[512,1024]{1,0:T(8,128)(2,1)S(1)}, bf16[512,1024]{1,0:T(8,128)(2,1)S(1)}, u32[]{:S(2)}, u32[]{:S(2)}) %collective-permute-start.4) | collective-permute-done | bytes 1048608 | tf_op jit(solution)/shard_map/ppermute | solution.py:90
  188.9 22.8 %collective-permute-done.5 = bf16[512,1024]{1,0:T(8,128)(2,1)} collective-permute-done((bf16[512,1024]{1,0:T(8,128)(2,1)S(1)}, bf16[512,1024]{1,0:T(8,128)(2,1)}, u32[]{:S(2)}, u32[]{:S(2)}) %collective-permute-start.5) | collective-permute-done | bytes 1048608 | tf_op jit(solution)/shard_map/ppermute | solution.py:90
  212.9 1.8 multiply_cosine_fusion
  214.6 19.9 %collective-permute-done.6 = bf16[512,1024]{1,0:T(8,128)(2,1)} collective-permute-done((bf16[512,1024]{1,0:T(8,128)(2,1)}, bf16[512,1024]{1,0:T(8,128)(2,1)}, u32[]{:S(2)}, u32[]{:S(2)}) %collective-permute-start.6) | collective-permute-done | bytes 1048608 | tf_op jit(solution)/shard_map/ppermute | solution.py:90
  237.2 1.3 constant_dynamic-update-slice_fusion.13
  239.8 1.3 constant_dynamic-update-slice_fusion.11
  244.7 5.7 %copy-done = bf16[512,16384]{1,0:T(8,128)(2,1)} copy-done((bf16[512,16384]{1,0:T(8,128)(2,1)}, bf16[512,16384]{1,0:T(8,128)(2,1)S(1)}, u32[]{:S(2)}) %copy-start) | copy-done | bytes 16777240
  250.4 1.7 fusion
  252.2 6.5 %convolution_bitcast_fusion = f32[512,1,128]{0,2,1:T(8,128)S(1)} fusion(bf16[8192,128]{1,0:T(8,128)(2,1)} %all-gather.7.cloned.1.call-done, f32[8192]{0:T(1024)S(1)} %copy-done.8, f32[512]{0:T(512)S(1)} %add_rsqrt_fusion, bf16[512,16384]{1,0:T(8,128)(2,1)} %copy-done, s32[]{:T(128)S(6)} %select_n.116), kind=kOutput, calls=%fused_computation.14 | convolution fusion | flops 1090519040 | bytes 10782724 | tf_op jit(solution)/shard_map/dot_general | solution.py:99
  259.4 7.0 %convolution_convert_fusion.2 = bf16[512,128]{1,0:T(8,128)(2,1)} fusion(bf16[8192,128]{1,0:T(8,128)(2,1)} %all-gather.5.cloned.1.call-done, f32[8192]{0:T(1024)S(1)} %copy-done.8, f32[512]{0:T(512)S(1)} %add_rsqrt_fusion, bf16[512,16384]{1,0:T(8,128)(2,1)} %copy-done, s32[]{:T(128)S(6)} %select_n.116), kind=kOutput, calls=%fused_computation.15 | convolution fusion | flops 1090584576 | bytes 10651652 | tf_op jit(solution)/shard_map/dot_general | solution.py:99
  266.5 11.6 %fusion.37 = f32[512,512]{0,1:T(8,128)S(1)} fusion(bf16[8192,512]{1,0:T(8,128)(2,1)} %all-gather.9.cloned.1.call-done, f32[8192]{0:T(1024)S(1)} %copy-done.8, f32[512]{0:T(512)S(1)} %add_rsqrt_fusion, bf16[512,16384]{1,0:T(8,128)(2,1)} %copy-done, s32[]{:T(128)S(6)} %select_n.116), kind=kOutput, calls=%fused_computation.107 | convolution fusion | flops 4311744512 | bytes 17860612 | tf_op jit(solution)/shard_map/dot_general | solution.py:99
  281.6 10.1 %convolution_convert_fusion = bf16[512,8192]{1,0:T(8,128)(2,1)} fusion(bf16[512,8192]{1,0:T(8,128)(2,1)} %all-gather.11.cloned.1.call-done, bf16[64,8,4,128]{3,2,1,0:T(4,128)(2,1)S(1)} %bitcast.86), kind=kOutput, calls=%fused_computation.8 | convolution fusion | flops 4299161600 | bytes 17301504 | tf_op jit(solution)/shard_map/dot_general | solution.py:128
  291.7 145.5 %reduce-scatter.2.cloned.1.call-done = bf16[512,1024]{1,0:T(8,128)(2,1)} async-done(((bf16[512,8192]{1,0:T(8,128)(2,1)}), bf16[512,1024]{1,0:T(8,128)(2,1)}) %reduce-scatter.2.cloned.1.call-update) | async-done | bytes 1048592 | tf_op jit(solution)/shard_map/reduce_scatter | solution.py:131
  (84 shorter events, 20.7 us)
Async XLA Ops:
  6.5 245.6 %all-gather.7.cloned.1.call-start = ((), (), s32[]{:S(2)}) async-start(), calls=%async_computation.3 | async-start | bytes 2621440 | tf_op jit(solution)/shard_map/all_gather | solution.py:102
  7.3 252.2 %all-gather.5.cloned.1.call-start = ((), (), s32[]{:S(2)}) async-start(), calls=%async_computation.2 | async-start | bytes 2621440 | tf_op jit(solution)/shard_map/all_gather | solution.py:103
  8.0 258.5 %all-gather.9.cloned.1.call-start = ((), (), s32[]{:S(2)}) async-start(), calls=%async_computation.4 | async-start | bytes 10485760 | tf_op jit(solution)/shard_map/all_gather | solution.py:101
  16.6 32.9 %all-to-all-start = ((bf16[4,192,1024]{2,1,0:T(8,128)(2,1)}), bf16[4,192,1024]{2,1,0:T(8,128)(2,1)S(1)}, u32[]{:S(2)}, u32[]{:S(2)}) async-start(bf16[4,192,1024]{2,1,0:T(8,128)(2,1)} %bitcast.6), calls=%async_computation | async-start | bytes 3145728 | tf_op jit(solution)/shard_map/all_to_all | solution.py:65
  20.9 260.7 %all-gather.11.cloned.1.call-start = ((), (), s32[]{:S(2)}) async-start(), calls=%async_computation.5 | async-start | bytes 10485760 | tf_op jit(solution)/shard_map/all_gather | solution.py:129
  55.5 27.7 %collective-permute-start = (bf16[512,1024]{1,0:T(8,128)(2,1)S(1)}, bf16[512,1024]{1,0:T(8,128)(2,1)S(1)}, u32[]{:S(2)}, u32[]{:S(2)}) collective-permute-start(bf16[512,1024]{1,0:T(8,128)(2,1)S(1)} %scatter_custom_fusion.2), channel_id=1, source_target_pairs={{0,1},{1,2},{2,3},{3,4},{4,5},{5,6},{6,7},{7,0},{8,9},{9,10},{10,1... | collective-permute-start | bytes 3145736 | tf_op jit(solution)/shard_map/ppermute | solution.py:90
  83.2 26.8 %collective-permute-start.1 = (bf16[512,1024]{1,0:T(8,128)(2,1)S(1)}, bf16[512,1024]{1,0:T(8,128)(2,1)S(1)}, u32[]{:S(2)}, u32[]{:S(2)}) collective-permute-start(bf16[512,1024]{1,0:T(8,128)(2,1)S(1)} %collective-permute-done), channel_id=1, source_target_pairs={{0,1},{1,2},{2,3},{3,4},{4,5},{5,6},{6,7},{7,0},{8,9},{9,10},{10,1... | collective-permute-start | bytes 3145736 | tf_op jit(solution)/shard_map/ppermute | solution.py:90
  83.2 354.0 %reduce-scatter.2.cloned.1.call-start = ((), (), s32[]{:S(2)}) async-start(), calls=%async_computation.6 | async-start | bytes 9437184 | tf_op jit(solution)/shard_map/reduce_scatter | solution.py:131
  110.0 25.9 %collective-permute-start.2 = (bf16[512,1024]{1,0:T(8,128)(2,1)S(1)}, bf16[512,1024]{1,0:T(8,128)(2,1)S(1)}, u32[]{:S(2)}, u32[]{:S(2)}) collective-permute-start(bf16[512,1024]{1,0:T(8,128)(2,1)S(1)} %collective-permute-done.1), channel_id=1, source_target_pairs={{0,1},{1,2},{2,3},{3,4},{4,5},{5,6},{6,7},{7,0},{8,9},{9,10},{10,1... | collective-permute-start | bytes 3145736 | tf_op jit(solution)/shard_map/ppermute | solution.py:90
  135.9 1.0 copy-start.1
  136.9 25.1 %collective-permute-start.3 = (bf16[512,1024]{1,0:T(8,128)(2,1)S(1)}, bf16[512,1024]{1,0:T(8,128)(2,1)S(1)}, u32[]{:S(2)}, u32[]{:S(2)}) collective-permute-start(bf16[512,1024]{1,0:T(8,128)(2,1)S(1)} %collective-permute-done.2), channel_id=1, source_target_pairs={{0,1},{1,2},{2,3},{3,4},{4,5},{5,6},{6,7},{7,0},{8,9},{9,10},{10,1... | collective-permute-start | bytes 3145736 | tf_op jit(solution)/shard_map/ppermute | solution.py:90
  162.0 1.0 copy-start.3
  163.0 24.2 %collective-permute-start.4 = (bf16[512,1024]{1,0:T(8,128)(2,1)S(1)}, bf16[512,1024]{1,0:T(8,128)(2,1)S(1)}, u32[]{:S(2)}, u32[]{:S(2)}) collective-permute-start(bf16[512,1024]{1,0:T(8,128)(2,1)S(1)} %collective-permute-done.3), channel_id=1, source_target_pairs={{0,1},{1,2},{2,3},{3,4},{4,5},{5,6},{6,7},{7,0},{8,9},{9,10},{10,1... | collective-permute-start | bytes 3145736 | tf_op jit(solution)/shard_map/ppermute | solution.py:90
  187.3 1.0 copy-start.5
  188.2 23.5 %collective-permute-start.5 = (bf16[512,1024]{1,0:T(8,128)(2,1)S(1)}, bf16[512,1024]{1,0:T(8,128)(2,1)}, u32[]{:S(2)}, u32[]{:S(2)}) collective-permute-start(bf16[512,1024]{1,0:T(8,128)(2,1)S(1)} %collective-permute-done.4), channel_id=1, source_target_pairs={{0,1},{1,2},{2,3},{3,4},{4,5},{5,6},{6,7},{7,0},{8,9},{9,10},{10,1... | collective-permute-start | bytes 3145736 | tf_op jit(solution)/shard_map/ppermute | solution.py:90
  211.7 22.8 %collective-permute-start.6 = (bf16[512,1024]{1,0:T(8,128)(2,1)}, bf16[512,1024]{1,0:T(8,128)(2,1)}, u32[]{:S(2)}, u32[]{:S(2)}) collective-permute-start(bf16[512,1024]{1,0:T(8,128)(2,1)} %collective-permute-done.5), channel_id=1, source_target_pairs={{0,1},{1,2},{2,3},{3,4},{4,5},{5,6},{6,7},{7,0},{8,9},{9,10},{10,1... | collective-permute-start | bytes 3145736 | tf_op jit(solution)/shard_map/ppermute | solution.py:90
  211.7 32.3 %copy-start.6 = (bf16[512,1024]{1,0:T(8,128)(2,1)S(1)}, bf16[512,1024]{1,0:T(8,128)(2,1)}, u32[]{:S(2)}) copy-start(bf16[512,1024]{1,0:T(8,128)(2,1)} %copy-done.5) | copy-start | bytes 3145732
  211.7 32.4 %copy-start.4 = (bf16[512,1024]{1,0:T(8,128)(2,1)S(1)}, bf16[512,1024]{1,0:T(8,128)(2,1)}, u32[]{:S(2)}) copy-start(bf16[512,1024]{1,0:T(8,128)(2,1)} %copy-done.3) | copy-start | bytes 3145732
  211.8 32.5 %copy-start.2 = (bf16[512,1024]{1,0:T(8,128)(2,1)S(1)}, bf16[512,1024]{1,0:T(8,128)(2,1)}, u32[]{:S(2)}) copy-start(bf16[512,1024]{1,0:T(8,128)(2,1)} %copy-done.1) | copy-start | bytes 3145732
  239.8 12.4 %copy-start.8 = (f32[8192]{0:T(1024)S(1)}, f32[8192]{0:T(1024)}, u32[]{:S(2)}) copy-start(f32[8192]{0:T(1024)} %param.10) | copy-start | bytes 98308
  244.7 5.7 %copy-start = (bf16[512,16384]{1,0:T(8,128)(2,1)}, bf16[512,16384]{1,0:T(8,128)(2,1)S(1)}, u32[]{:S(2)}) copy-start(bf16[512,16384]{1,0:T(8,128)(2,1)S(1)} %constant_dynamic-update-slice_fusion) | copy-start | bytes 50331652
  266.5 12.4 %copy-start.7 = (f32[512,64]{1,0:T(8,128)S(1)}, f32[512,64]{1,0:T(8,128)}, u32[]{:S(2)}) copy-start(f32[512,64]{1,0:T(8,128)} %get-tuple-element.16) | copy-start | bytes 393220
Sparse Core Ops, SparseCore 0:
  8.9 33.8 all-gather.6
  44.3 21.8 all-gather.4
  67.8 58.2 all-gather.8
  127.5 58.2 all-gather.10
  291.8 145.3 reduce-scatter.1
